TPU v7x, 512 devices: a whole 4x8x8 slice. The times are simulated.
512 devices in a mesh: dp: 256 (over z, y, x), ctx: 2 (over core).
Axes of the slice: x: 4, y: 8, z: 8, core: 2. Of those that a mesh axis runs over, the one named last changes fastest.
Arguments:
- head_inputs: bfloat16 [256, 512, 1024], P('dp', 'ctx'), may hold values from -6 to 6
- cotangent: bfloat16 [256, 512, 1024], P('dp', 'ctx'), may hold values from -6 to 6
- write_proj: bfloat16 [256, 512, 256], P('dp', 'ctx'), may hold values from -3 to 3
- read_proj: bfloat16 [256, 512, 256], P('dp', 'ctx'), may hold values from -3 to 3
- step_raw: float32 [256, 512, 16], P('dp', 'ctx'), may hold values from -4 to 4
- doc_index: int32 [256, 512], P('dp', 'ctx'), may hold values from 0 to 15, never falling along the last dimension, each value on 1 to 257 neighbouring positions
- log_rate: float32 [16], replicated, may hold values from 0 to 2.77
- step_bias: float32 [16], replicated, may hold values from -6.9 to -2.25
- skip_gain: float32 [16], replicated, may hold values from 0.5 to 1.5
Outputs:
- grad_inputs: bfloat16 [256, 512, 1024], P('dp', 'ctx')
- grad_write: bfloat16 [256, 512, 256], P('dp', 'ctx')
- grad_read: bfloat16 [256, 512, 256], P('dp', 'ctx')
- grad_step: float32 [256, 512, 16], P('dp', 'ctx')
- grad_rate: float32 [16], replicated
- grad_bias: float32 [16], replicated
- grad_skip: float32 [16], replicated
Inputs may be any that keep to these rules, and one draw needn't show every extreme that they name: doc_index never falls along a sequence; each document spans 1 to 257 tokens and one of each sequence spans exactly that many.
All inputs are finite; a program needn't handle non-finite values.
Results may differ from a plain program's by a relative error of at most 0.0025.
Values may be sent and summed in bfloat16 or wider, within the bound.
No kernel may reach another device: no remote copies, remote signals or barrier semaphores. Data moves between devices by JAX's collectives and lax.ppermute only.
A program may use at most 64 MiB of HBM per device.

v0:
```python
import jax
import jax.numpy as jnp
from jax import lax
from jax.sharding import PartitionSpec as P

HEADS = 16
HEAD_DIM = 64
STATE = 256
BLOCK = 256


def ssd_forward(
    inputs, writes, reads, steps, segment, segment_prev, state_init, log_rate, skip_gain
):
    length, heads, width = inputs.shape
    count = length // BLOCK
    rate_all = steps * (-jnp.exp(log_rate))[None, :]
    blocks = (
        inputs.reshape(count, BLOCK, heads, width),
        writes.reshape(count, BLOCK, -1),
        reads.reshape(count, BLOCK, -1),
        steps.reshape(count, BLOCK, heads),
        rate_all.reshape(count, BLOCK, heads),
        segment.reshape(count, BLOCK),
    )
    causal = jnp.arange(BLOCK)[:, None] >= jnp.arange(BLOCK)[None, :]
    highest = lax.Precision.HIGHEST

    def advance(carry, piece):
        state, last_doc = carry
        in_block, write_block, read_block, step_block, rate_block, doc_block = piece
        cumulative = jnp.cumsum(rate_block, axis=0)
        same_doc = causal & (doc_block[:, None] == doc_block[None, :])
        gaps = cumulative[:, None, :] - cumulative[None, :, :]
        decay = jnp.exp(jnp.where(same_doc[:, :, None], gaps, -1e30))
        scores = jnp.einsum("in,jn->ij", read_block, write_block, precision=highest)
        mixing = decay * (scores[:, :, None] * step_block[None, :, :])
        result = jnp.einsum("ijh,jhp->ihp", mixing, in_block, precision=highest)
        keep = (doc_block == last_doc).astype(jnp.float32)
        start = jnp.exp(cumulative) * keep[:, None]
        result = (
            result
            + jnp.einsum("in,hpn->ihp", read_block, state, precision=highest) * start[:, :, None]
        )
        result = result + skip_gain[None, :, None] * in_block
        end_doc = doc_block[BLOCK - 1]
        tail = (
            jnp.exp(cumulative[BLOCK - 1][None, :] - cumulative)
            * (doc_block == end_doc).astype(jnp.float32)[:, None]
            * step_block
        )
        carried = jnp.exp(cumulative[BLOCK - 1]) * (end_doc == last_doc).astype(jnp.float32)
        state = carried[:, None, None] * state + jnp.einsum(
            "jh,jhp,jn->hpn", tail, in_block, write_block, precision=highest
        )
        return ((state, end_doc), result)

    (state, _), results = lax.scan(jax.checkpoint(advance), (state_init, segment_prev), blocks)
    return (results.reshape(length, heads, width), state)


def layer_grads(
    inputs,
    cotangent,
    writes,
    reads,
    step_raw,
    segment,
    segment_prev,
    state_init,
    log_rate,
    step_bias,
    skip_gain,
    state_grad,
):
    length = inputs.shape[0]
    heads = step_raw.shape[1]
    head_view = inputs.astype(jnp.float32).reshape(length, heads, HEAD_DIM)

    def forward(head_view, writes, reads, step_raw, log_rate, step_bias, skip_gain):
        steps = jax.nn.softplus(step_raw + step_bias[None, :])
        return ssd_forward(
            head_view, writes, reads, steps, segment, segment_prev, state_init, log_rate, skip_gain
        )

    _, pullback = jax.vjp(
        forward,
        head_view,
        writes.astype(jnp.float32),
        reads.astype(jnp.float32),
        step_raw,
        log_rate,
        step_bias,
        skip_gain,
    )
    return pullback((cotangent.astype(jnp.float32).reshape(length, heads, HEAD_DIM), state_grad))


def on_device(
    head_inputs,
    cotangent,
    write_proj,
    read_proj,
    step_raw,
    doc_index,
    log_rate,
    step_bias,
    skip_gain,
):
    group_size = lax.axis_size("ctx")
    per_device = HEADS // group_size
    first_head = lax.axis_index("ctx") * per_device
    head_rows, cotan_rows = (
        lax.all_to_all(head_inputs, "ctx", split_axis=2, concat_axis=1, tiled=True),
        lax.all_to_all(cotangent, "ctx", split_axis=2, concat_axis=1, tiled=True),
    )
    raw_steps = lax.all_to_all(step_raw, "ctx", split_axis=2, concat_axis=1, tiled=True)
    write_all, read_all = (
        lax.all_gather(write_proj, "ctx", axis=1, tiled=True),
        lax.all_gather(read_proj, "ctx", axis=1, tiled=True),
    )
    segment = lax.all_gather(doc_index, "ctx", axis=1, tiled=True)[0]
    length = segment.shape[0]
    rate_here = lax.dynamic_slice_in_dim(log_rate, first_head, per_device)
    bias_here = lax.dynamic_slice_in_dim(step_bias, first_head, per_device)
    skip_here = lax.dynamic_slice_in_dim(skip_gain, first_head, per_device)
    zero_state = jnp.zeros((per_device, HEAD_DIM, STATE), jnp.float32)
    grads = layer_grads(
        head_rows[0],
        cotan_rows[0],
        write_all[0],
        read_all[0],
        raw_steps[0],
        segment,
        segment[0],
        zero_state,
        rate_here,
        bias_here,
        skip_here,
        zero_state,
    )
    out_inputs = lax.all_to_all(
        grads[0].reshape(1, length, per_device * HEAD_DIM).astype(jnp.bfloat16),
        "ctx",
        split_axis=1,
        concat_axis=2,
        tiled=True,
    )
    out_step = lax.all_to_all(grads[3][None], "ctx", split_axis=1, concat_axis=2, tiled=True)
    sum_write, sum_read = (
        lax.psum_scatter(grads[1][None], "ctx", scatter_dimension=1, tiled=True),
        lax.psum_scatter(grads[2][None], "ctx", scatter_dimension=1, tiled=True),
    )
    out_write = sum_write.astype(jnp.bfloat16)
    out_read = sum_read.astype(jnp.bfloat16)

    def place(values):
        return lax.dynamic_update_slice_in_dim(
            jnp.zeros((HEADS,), jnp.float32), values, first_head, 0
        )

    partial_sums = (place(grads[4]), place(grads[5]), place(grads[6]))
    total_rate, total_bias, total_skip = lax.psum(
        (partial_sums[0], partial_sums[1], partial_sums[2]), ("dp", "ctx")
    )
    return (out_inputs, out_write, out_read, out_step, total_rate, total_bias, total_skip)


def solution(mesh):
    placed = (
        P("dp", "ctx", None),
        P("dp", "ctx", None),
        P("dp", "ctx", None),
        P("dp", "ctx", None),
        P("dp", "ctx", None),
        P("dp", "ctx"),
        P(),
        P(),
        P(),
    )
    return jax.shard_map(
        on_device,
        mesh=mesh,
        in_specs=placed,
        out_specs=(
            P("dp", "ctx", None),
            P("dp", "ctx", None),
            P("dp", "ctx", None),
            P("dp", "ctx", None),
            P(),
            P(),
            P(),
        ),
        check_vma=False,
    )
```

profile of v0, /device:TPU:1, one launch (start us, length us, event | category | flops | bytes accessed | tf_op | source)
XLA Modules:
  0.0 267.5 jit_solution(3828304413454677464)
XLA Ops:
  7.2 2.4 copy.57
  10.2 3.9 %reduce.18 = bf16[1024,256]{1,0:T(8,128)(2,1)S(1)} reduce(bf16[1024,1,256]{2,1,0:T(2,128)(2,1)S(1)} %bitcast.276, bf16[]{:T(256)} %broadcast.266), dimensions={1}, to_apply=%bitcast.160.reduce_sub_computation | reduce | bytes 1048578
  15.0 10.5 %all-to-all-start.1 = ((bf16[2,2,65536]{2,1,0:T(2,128)(2,1)}), bf16[2,2,65536]{2,1,0:T(2,128)(2,1)S(1)}, u32[]{:S(2)}, u32[]{:S(2)}) async-start(bf16[2,2,65536]{2,1,0:T(2,128)(2,1)} %reshape.420), calls=%async_computation.1 | async-start | bytes 1048576 | tf_op jit(solution)/shard_map/all_to_all | solution.py:114
  30.4 2.0 all_gather.10
  32.4 2.0 all_gather.11
  34.4 2.4 copy.58
  36.8 4.7 %reduce.19 = bf16[1024,256]{1,0:T(8,128)(2,1)} reduce(bf16[1024,1,256]{2,1,0:T(2,128)(2,1)S(1)} %bitcast.280, bf16[]{:T(256)} %broadcast.266), dimensions={1}, to_apply=%bitcast.162.reduce_sub_computation | reduce | bytes 1048578
  41.5 1.8 reshape.422
  43.3 4.4 %all-to-all-start.2 = ((bf16[2,2,65536]{2,1,0:T(2,128)(2,1)}), bf16[2,2,65536]{2,1,0:T(2,128)(2,1)}, u32[]{:S(2)}, u32[]{:S(2)}) async-start(bf16[2,2,65536]{2,1,0:T(2,128)(2,1)} %reshape.422), calls=%async_computation.2 | async-start | bytes 1048576 | tf_op jit(solution)/shard_map/all_to_all | solution.py:115
  50.4 3.3 %all-to-all-start = ((f32[1,256,16]{1,0,2:T(1,128)}), f32[1,256,16]{1,0,2:T(1,128)S(1)}, u32[]{:S(2)}, u32[]{:S(2)}) async-start(f32[1,256,16]{1,0,2:T(1,128)} %copy.56), calls=%async_computation | async-start | bytes 32768 | tf_op jit(solution)/shard_map/all_to_all | solution.py:117
  58.1 13.2 %while.44 = (s32[]{:T(128)}, f32[8,64,256]{2,1,0:T(8,128)S(1)}, s32[]{:T(128)}, f32[2,8,64,256]{3,2,1,0:T(8,128)}, s32[2]{0:T(128)S(1)}, /*index=5*/f32[2,256,8]...) while((s32[]{:T(128)}, f32[8,64,256]{2,1,0:T(8,128)S(1)}, ...), condition=%wide.region_3.4_spmd.clone, body=%wide.region_0.3_spmd.clone.sunk | while | flops 403577376 | bytes 2971505 | solution.py:58
  62.8 1.9 convolution_add_fusion.6
  69.4 1.9 convolution_add_fusion.6
  75.0 60.5 %while.45 = (s32[]{:T(128)}, f32[8]{0:T(128)}, f32[8,64,256]{2,1,0:T(8,128)}, bf16[2,256,8,64]{1,3,2,0:T(8,128)(2,1)}, f32[2,256,256]{2,1,0:T(8,128)}, /*index=5...) while((s32[]{:T(128)}, f32[8]{0:T(128)}, ...), condition=%wide.region_17.18_spmd.clone, body=%wide.region_4.0_spmd.clone.sunk | while | flops 3434652672 | bytes 35708892 | solution.py:58
  86.1 4.1 %fusion.109 = (f32[256,8]{0,1:T(8,128)}, f32[256,8]{0,1:T(8,128)}, f32[256,8]{0,1:T(8,128)}, f32[256,256]{1,0:T(8,128)S(1)}) fusion(f32[256,8]{0,1:T(8,128)S(1)} %get-tuple-element.914, f32[256,256]{1,0:T(8,128)S(1)} %fusion.108, f32[256,8]{0,1:T(8,128)S(1)} %get-tuple-element.912, pred[256,256]{1,0:T(8,128)(4,1)S(1)} %compare_and_fusion.2, ...), kind=kOutput, calls=%fused_computation.30.clone.1 | convolution fusion | flops 409397248 | bytes 1679360 | tf_op jit(solution)/shard_map/transpose(jvp())/while/body/eval_jaxpr/checkpoint/ijh,jhp->ihp/dot_general | solution.py:38
  94.8 3.6 %fusion.112 = bf16[2,256,8,64]{1,3,2,0:T(8,128)(2,1)} fusion(bf16[2,256,8,64]{1,3,2,0:T(8,128)(2,1)} %get-tuple-element.993, s32[]{:T(128)S(6)} %sub.194, f32[256,8]{0,1:T(8,128)S(1)} %get-tuple-element.914, f32[256,256]{1,0:T(8,128)} %copy-done.1, f32[256,8]{0,1:T(8,128)S(1)} %get-tuple-element.912, pred[256,256]{1,0:T(8,128)(4,1)S(1)} %compare_and_fusion.2, ...), kind=kOutput, calls=%fused_computation.33.clone.1 | convolution fusion | flops 405274624 | bytes 2458116 | tf_op jit(solution)/shard_map/transpose(jvp())/while/body/eval_jaxpr/checkpoint/ijh,jhp->ihp/dot_general | solution.py:38
  101.4 2.5 reduce-window.70
  116.9 4.0 %fusion.109 = (f32[256,8]{0,1:T(8,128)}, f32[256,8]{0,1:T(8,128)}, f32[256,8]{0,1:T(8,128)}, f32[256,256]{1,0:T(8,128)S(1)}) fusion(f32[256,8]{0,1:T(8,128)S(1)} %get-tuple-element.914, f32[256,256]{1,0:T(8,128)S(1)} %fusion.108, f32[256,8]{0,1:T(8,128)S(1)} %get-tuple-element.912, pred[256,256]{1,0:T(8,128)(4,1)S(1)} %compare_and_fusion.2, ...), kind=kOutput, calls=%fused_computation.30.clone.1 | convolution fusion | flops 409397248 | bytes 1679360 | tf_op jit(solution)/shard_map/transpose(jvp())/while/body/eval_jaxpr/checkpoint/ijh,jhp->ihp/dot_general | solution.py:38
  125.5 3.6 %fusion.112 = bf16[2,256,8,64]{1,3,2,0:T(8,128)(2,1)} fusion(bf16[2,256,8,64]{1,3,2,0:T(8,128)(2,1)} %get-tuple-element.993, s32[]{:T(128)S(6)} %sub.194, f32[256,8]{0,1:T(8,128)S(1)} %get-tuple-element.914, f32[256,256]{1,0:T(8,128)} %copy-done.1, f32[256,8]{0,1:T(8,128)S(1)} %get-tuple-element.912, pred[256,256]{1,0:T(8,128)(4,1)S(1)} %compare_and_fusion.2, ...), kind=kOutput, calls=%fused_computation.33.clone.1 | convolution fusion | flops 405274624 | bytes 2458116 | tf_op jit(solution)/shard_map/transpose(jvp())/while/body/eval_jaxpr/checkpoint/ijh,jhp->ihp/dot_general | solution.py:38
  132.2 2.5 reduce-window.70
  140.1 3.3 %all-to-all-start.4 = ((f32[2,1,2048]{2,1,0:T(1,128)}), f32[2,1,2048]{2,1,0:T(1,128)S(1)}, u32[]{:S(2)}, u32[]{:S(2)}) async-start(f32[2,1,2048]{2,1,0:T(1,128)} %reshape.426), calls=%async_computation.6 | async-start | bytes 32768 | tf_op jit(solution)/shard_map/all_to_all | solution.py:149
  143.4 99.9 %all-reduce.2 = (f32[16]{0:T(128)}, f32[16]{0:T(128)}, f32[16]{0:T(128)}) all-reduce(f32[16]{0:T(128)S(1)} %multiply_dynamic-update-slice_fusion, f32[16]{0:T(128)S(1)} %dynamic_update_slice.66, f32[16]{0:T(128)S(1)} %dynamic_update_slice.67), channel_id=1, replica_groups=mesh['dp'=256,'ctx'=2] {'dp','ctx'}, use_global_device_ids=true, to_apply=%region_21.22 | all-reduce | flops 48 | bytes 384 | tf_op jit(solution)/shard_map/psum | solution.py:163
  244.6 3.9 %reduce.20 = bf16[512,512]{1,0:T(8,128)(2,1)S(1)} reduce(bf16[512,1,512]{2,1,0:T(2,128)(2,1)S(1)} %bitcast.277, bf16[]{:T(256)} %broadcast.266), dimensions={1}, to_apply=%bitcast.164.reduce_sub_computation | reduce | bytes 1048578
  249.5 4.2 %all-to-all-start.3 = ((bf16[2,2,65536]{2,1,0:T(2,128)(2,1)}), bf16[2,2,65536]{2,1,0:T(2,128)(2,1)S(1)}, u32[]{:S(2)}, u32[]{:S(2)}) async-start(bf16[2,2,65536]{2,1,0:T(2,128)(2,1)} %reshape.424), calls=%async_computation.3 | async-start | bytes 1048576 | tf_op jit(solution)/shard_map/all_to_all | solution.py:142
  (276 shorter events, 74.8 us)
Async XLA Ops:
  14.0 11.4 %copy-start.32 = (f32[16]{0:T(128)S(1)}, f32[16]{0:T(128)}, u32[]{:S(2)}) copy-start(f32[16]{0:T(128)} %param.20) | copy-start | bytes 196
  14.1 11.5 %copy-start.30 = (f32[16]{0:T(128)S(1)}, f32[16]{0:T(128)}, u32[]{:S(2)}) copy-start(f32[16]{0:T(128)} %param.19) | copy-start | bytes 196
  14.1 11.6 %copy-start.33 = (f32[16]{0:T(128)S(1)}, f32[16]{0:T(128)}, u32[]{:S(2)}) copy-start(f32[16]{0:T(128)} %param.21) | copy-start | bytes 196
  14.1 12.2 %copy-start.29 = (s32[1,256]{1,0:T(1,128)S(1)}, s32[1,256]{1,0:T(1,128)}, u32[]{:S(2)}) copy-start(s32[1,256]{1,0:T(1,128)} %param.18) | copy-start | bytes 3076
  14.1 15.6 %copy-start.20 = (f32[1,256,16]{1,2,0:T(8,128)S(1)}, f32[1,256,16]{1,2,0:T(8,128)}, u32[]{:S(2)}) copy-start(f32[1,256,16]{1,2,0:T(8,128)} %param.17) | copy-start | bytes 49156
  14.1 16.3 %copy-start.16 = (bf16[1,256,256]{2,1,0:T(8,128)(2,1)S(1)}, bf16[1,256,256]{2,1,0:T(8,128)(2,1)}, u32[]{:S(2)}) copy-start(bf16[1,256,256]{2,1,0:T(8,128)(2,1)} %param.15) | copy-start | bytes 393220
  15.0 17.4 %copy-start.17 = (bf16[1,256,256]{2,1,0:T(8,128)(2,1)S(1)}, bf16[1,256,256]{2,1,0:T(8,128)(2,1)}, u32[]{:S(2)}) copy-start(bf16[1,256,256]{2,1,0:T(8,128)(2,1)} %param.16) | copy-start | bytes 393220
  15.0 28.3 %all-to-all-start.1 = ((bf16[2,2,65536]{2,1,0:T(2,128)(2,1)}), bf16[2,2,65536]{2,1,0:T(2,128)(2,1)S(1)}, u32[]{:S(2)}, u32[]{:S(2)}) async-start(bf16[2,2,65536]{2,1,0:T(2,128)(2,1)} %reshape.420), calls=%async_computation.1 | async-start | bytes 1048576 | tf_op jit(solution)/shard_map/all_to_all | solution.py:114
  25.6 31.9 %copy-start.25 = (f32[8]{0:T(128)}, f32[8]{0:T(128)S(1)}, u32[]{:S(2)}) copy-start(f32[8]{0:T(128)S(1)} %dynamic_slice.111) | copy-start | bytes 100
  25.6 31.8 %copy-start.27 = (f32[8]{0:T(128)}, f32[8]{0:T(128)S(1)}, u32[]{:S(2)}) copy-start(f32[8]{0:T(128)S(1)} %fusion.50) | copy-start | bytes 100
  43.3 7.0 %all-to-all-start.2 = ((bf16[2,2,65536]{2,1,0:T(2,128)(2,1)}), bf16[2,2,65536]{2,1,0:T(2,128)(2,1)}, u32[]{:S(2)}, u32[]{:S(2)}) async-start(bf16[2,2,65536]{2,1,0:T(2,128)(2,1)} %reshape.422), calls=%async_computation.2 | async-start | bytes 1048576 | tf_op jit(solution)/shard_map/all_to_all | solution.py:115
  50.4 7.1 %all-to-all-start = ((f32[1,256,16]{1,0,2:T(1,128)}), f32[1,256,16]{1,0,2:T(1,128)S(1)}, u32[]{:S(2)}, u32[]{:S(2)}) async-start(f32[1,256,16]{1,0,2:T(1,128)} %copy.56), calls=%async_computation | async-start | bytes 32768 | tf_op jit(solution)/shard_map/all_to_all | solution.py:117
  53.6 203.8 %reduce-scatter.3.cloned.1.call-start = ((), (), s32[]{:S(2)}) async-start(), calls=%async_computation.7 | async-start | bytes 786432 | tf_op jit(solution)/shard_map/reduce_scatter | solution.py:151
  82.4 9.5 %copy-start.7 = (f32[256]{0:T(256)}, f32[256]{0:T(256)S(1)}, u32[]{:S(2)}) copy-start(f32[256]{0:T(256)S(1)} %get-tuple-element.920) | copy-start | bytes 3076 | tf_op jit(solution)/shard_map/transpose(jvp())/while
  83.5 8.5 %copy-start.11 = (f32[8]{0:T(128)}, f32[8]{0:T(128)S(1)}, u32[]{:S(2)}) copy-start(f32[8]{0:T(128)S(1)} %get-tuple-element.913) | copy-start | bytes 100 | tf_op jit(solution)/shard_map/transpose(jvp())/while
  99.4 5.3 %copy-start.19 = (s32[2,256]{1,0:T(2,128)S(1)}, s32[2,256]{1,0:T(2,128)}, u32[]{:S(2)}) copy-start(s32[2,256]{1,0:T(2,128)} %copy-done.18) | copy-start | bytes 6148 | tf_op jit(solution)/shard_map/transpose(jvp())/while
  99.4 5.3 %copy-start.35 = (s32[2]{0:T(128)S(1)}, s32[2]{0:T(128)}, u32[]{:S(2)}) copy-start(s32[2]{0:T(128)} %copy-done.34) | copy-start | bytes 28 | tf_op jit(solution)/shard_map/transpose(jvp())/while
  113.2 9.5 %copy-start.7 = (f32[256]{0:T(256)}, f32[256]{0:T(256)S(1)}, u32[]{:S(2)}) copy-start(f32[256]{0:T(256)S(1)} %get-tuple-element.920) | copy-start | bytes 3076 | tf_op jit(solution)/shard_map/transpose(jvp())/while
  114.3 8.4 %copy-start.11 = (f32[8]{0:T(128)}, f32[8]{0:T(128)S(1)}, u32[]{:S(2)}) copy-start(f32[8]{0:T(128)S(1)} %get-tuple-element.913) | copy-start | bytes 100 | tf_op jit(solution)/shard_map/transpose(jvp())/while
  130.1 5.3 %copy-start.19 = (s32[2,256]{1,0:T(2,128)S(1)}, s32[2,256]{1,0:T(2,128)}, u32[]{:S(2)}) copy-start(s32[2,256]{1,0:T(2,128)} %copy-done.18) | copy-start | bytes 6148 | tf_op jit(solution)/shard_map/transpose(jvp())/while
  135.6 107.7 %copy-start.4 = (bf16[2,256,8,64]{1,3,2,0:T(8,128)(2,1)S(1)}, bf16[2,256,8,64]{1,3,2,0:T(8,128)(2,1)}, u32[]{:S(2)}) copy-start(bf16[2,256,8,64]{1,3,2,0:T(8,128)(2,1)} %get-tuple-element.448) | copy-start | bytes 1572868
  135.6 123.4 %reduce-scatter.5.cloned.1.call-start = ((), (), s32[]{:S(2)}) async-start(), calls=%async_computation.8 | async-start | bytes 786432 | tf_op jit(solution)/shard_map/reduce_scatter | solution.py:152
  140.1 109.4 %all-to-all-start.4 = ((f32[2,1,2048]{2,1,0:T(1,128)}), f32[2,1,2048]{2,1,0:T(1,128)S(1)}, u32[]{:S(2)}, u32[]{:S(2)}) async-start(f32[2,1,2048]{2,1,0:T(1,128)} %reshape.426), calls=%async_computation.6 | async-start | bytes 32768 | tf_op jit(solution)/shard_map/all_to_all | solution.py:149
  249.5 6.0 %all-to-all-start.3 = ((bf16[2,2,65536]{2,1,0:T(2,128)(2,1)}), bf16[2,2,65536]{2,1,0:T(2,128)(2,1)S(1)}, u32[]{:S(2)}, u32[]{:S(2)}) async-start(bf16[2,2,65536]{2,1,0:T(2,128)(2,1)} %reshape.424), calls=%async_computation.3 | async-start | bytes 1048576 | tf_op jit(solution)/shard_map/all_to_all | solution.py:142
  (37 other events, 78.1 us)
Sparse Core Ops, SparseCore 0:
  135.7 16.2 reduce-scatter.2
  155.1 17.3 reduce-scatter.4
where the time goes:
time: 269 us; the launch traced here: 267 us
  blocking collectives  106 us (39%)
  other arithmetic  44.1 us (16%)
  local copies, waits for them, and re-layouts  38.4 us (14%)
  matrix products  32.5 us (12%)
  starting transfers between devices  26 us (10%)
  between operations  14.4 us (5%)
  loops' own time  5.8 us (2%)
    psum x1, blocking collectives, on_device(): lax.psum((partial_sums[0], partial_sums[1], partial_sums[2]), ('dp', 'ctx'))  99.9 us
    unnamed x54, local copies, waits for them, and re-layouts  17.9 us
    dot_general x4, matrix products, advance(): result = jnp.einsum('ijh,jhp->ihp', mixing, in_block, precision=highest)  15.2 us
    unnamed x7, other arithmetic  13.7 us
    all_to_all x1, starting transfers between devices, on_device(): lax.all_to_all(head_inputs, 'ctx', split_axis=2, concat_axis=1, tiled=True)  10.5 us
    another operation x17, other arithmetic  9.32 us
    dot_general x6, matrix products, advance(): jnp.einsum('jh,jhp,jn->hpn', tail, in_block, write_block, precision=highest)  7.06 us
    dot_general x6, matrix products, advance(): jnp.einsum('in,hpn->ihp', read_block, state, precision=highest)  6.04 us
  transfers between devices with their start and end apart: 7, of which 0 were waited for; matrix products, arithmetic and copies ran while one was open for 12% of the time, Pallas kernels for 0%

commit v1 on v0

--- a/solution.py
+++ b/solution.py
@@ -7,6 +7,11 @@
 HEAD_DIM = 64
 STATE = 256
 BLOCK = 256
+
+
+def axis_by_axis(x, one, other):
+    inner = lax.psum(x, one)
+    return lax.psum(inner, other)
 
 
 def ssd_forward(
@@ -160,8 +165,8 @@
         )
 
     partial_sums = (place(grads[4]), place(grads[5]), place(grads[6]))
-    total_rate, total_bias, total_skip = lax.psum(
-        (partial_sums[0], partial_sums[1], partial_sums[2]), ("dp", "ctx")
+    total_rate, total_bias, total_skip = axis_by_axis(
+        (partial_sums[0], partial_sums[1], partial_sums[2]), "dp", "ctx"
     )
     return (out_inputs, out_write, out_read, out_step, total_rate, total_bias, total_skip)
 

time: 269 us -> 863 us (3.21)
  blocking collectives: 106 us -> 700 us
    psum x1 -> x2, blocking collectives: 99.9 us -> 694 us  [the longest x1 581 us: axis_by_axis(): inner = lax.psum(x, one)]
  transfers between devices with their start and end apart: 7 -> 7, of which waited for: 0 -> 0; matrix products, arithmetic and copies ran while one was open for 12% -> 4% of each run, Pallas kernels for 0% -> 0%
where the time goes in v1:
time: 863 us; the launch traced here: 861 us
  blocking collectives  700 us (81%)
  other arithmetic  44.1 us (5%)
  local copies, waits for them, and re-layouts  38.4 us (4%)
  matrix products  32.5 us (4%)
  starting transfers between devices  25.4 us (3%)
  between operations  14.4 us (2%)
    psum x1, blocking collectives, axis_by_axis(): inner = lax.psum(x, one)  581 us
    psum x1, blocking collectives, axis_by_axis(): return lax.psum(inner, other)  113 us
    unnamed x54, local copies, waits for them, and re-layouts  17.9 us
  transfers between devices with their start and end apart: 7, of which 0 were waited for; matrix products, arithmetic and copies ran while one was open for 4% of the time, Pallas kernels for 0%

profile of v1, /device:TPU:1, one launch (start us, length us, event | category | flops | bytes accessed | tf_op | source)
XLA Modules:
  0.0 861.5 jit_solution(13816192471839117244)
XLA Ops:
  7.2 2.4 copy.57
  10.2 3.9 reduce.18
  15.0 10.5 %all-to-all-start.1 = ((bf16[2,2,65536]{2,1,0:T(2,128)(2,1)}), bf16[2,2,65536]{2,1,0:T(2,128)(2,1)S(1)}, u32[]{:S(2)}, u32[]{:S(2)}) async-start(bf16[2,2,65536]{2,1,0:T(2,128)(2,1)} %reshape.420), calls=%async_computation.1 | async-start | bytes 1048576 | tf_op jit(solution)/shard_map/all_to_all | solution.py:119
  30.4 2.0 all_gather.10
  32.4 2.0 all_gather.11
  34.4 2.4 copy.58
  36.8 4.7 reduce.19
  43.3 4.4 all-to-all-start.2
  50.4 3.3 all-to-all-start
  58.1 13.2 %while.44 = (s32[]{:T(128)}, f32[8,64,256]{2,1,0:T(8,128)S(1)}, s32[]{:T(128)}, f32[2,8,64,256]{3,2,1,0:T(8,128)}, s32[2]{0:T(128)S(1)}, /*index=5*/f32[2,256,8]...) while((s32[]{:T(128)}, f32[8,64,256]{2,1,0:T(8,128)S(1)}, ...), condition=%wide.region_3.4_spmd.clone, body=%wide.region_0.3_spmd.clone.sunk | while | flops 403577376 | bytes 2971505 | solution.py:63
  62.8 1.9 convolution_add_fusion.6
  69.4 1.9 convolution_add_fusion.6
  75.0 60.5 %while.45 = (s32[]{:T(128)}, f32[8]{0:T(128)}, f32[8,64,256]{2,1,0:T(8,128)}, bf16[2,256,8,64]{1,3,2,0:T(8,128)(2,1)}, f32[2,256,256]{2,1,0:T(8,128)}, /*index=5...) while((s32[]{:T(128)}, f32[8]{0:T(128)}, ...), condition=%wide.region_17.18_spmd.clone, body=%wide.region_4.0_spmd.clone.sunk | while | flops 3434652672 | bytes 35708892 | solution.py:63
  86.1 4.1 fusion.109
  94.8 3.6 fusion.112
  101.4 2.5 reduce-window.70
  116.9 4.0 fusion.109
  125.5 3.6 fusion.112
  132.2 2.5 reduce-window.70
  139.2 3.5 all-to-all-start.4
  144.0 3.9 reduce.20
  148.9 3.5 all-to-all-start.3
  157.0 581.2 %all-reduce.2 = (f32[16]{0:T(128)S(1)}, f32[16]{0:T(128)S(1)}, f32[16]{0:T(128)S(1)}) all-reduce(f32[16]{0:T(128)S(1)} %multiply_dynamic-update-slice_fusion, f32[16]{0:T(128)S(1)} %dynamic_update_slice.66, f32[16]{0:T(128)S(1)} %dynamic_update_slice.67), channel_id=1, replica_groups=mesh['dp'=256,'ctx'=2] {'dp'}, use_global_device_ids=true, to_apply=%region_21.22 | all-reduce | flops 48 | bytes 384 | tf_op jit(solution)/shard_map/psum | solution.py:13
  738.2 113.2 %all-reduce.3 = (f32[16]{0:T(128)}, f32[16]{0:T(128)}, f32[16]{0:T(128)}) all-reduce(f32[16]{0:T(128)S(1)} %get-tuple-element.671, f32[16]{0:T(128)S(1)} %get-tuple-element.672, f32[16]{0:T(128)S(1)} %get-tuple-element.673), channel_id=1, replica_groups=mesh['dp'=256,'ctx'=2] {'ctx'}, use_global_device_ids=true, to_apply=%region_22.23 | all-reduce | flops 48 | bytes 384 | tf_op jit(solution)/shard_map/psum | solution.py:14
  (277 shorter events, 76.6 us)
Async XLA Ops:
  14.0 11.4 %copy-start.32 = (f32[16]{0:T(128)S(1)}, f32[16]{0:T(128)}, u32[]{:S(2)}) copy-start(f32[16]{0:T(128)} %param.20) | copy-start | bytes 196
  14.1 11.5 %copy-start.30 = (f32[16]{0:T(128)S(1)}, f32[16]{0:T(128)}, u32[]{:S(2)}) copy-start(f32[16]{0:T(128)} %param.19) | copy-start | bytes 196
  14.1 11.6 %copy-start.33 = (f32[16]{0:T(128)S(1)}, f32[16]{0:T(128)}, u32[]{:S(2)}) copy-start(f32[16]{0:T(128)} %param.21) | copy-start | bytes 196
  14.1 12.2 %copy-start.29 = (s32[1,256]{1,0:T(1,128)S(1)}, s32[1,256]{1,0:T(1,128)}, u32[]{:S(2)}) copy-start(s32[1,256]{1,0:T(1,128)} %param.18) | copy-start | bytes 3076
  14.1 15.6 %copy-start.20 = (f32[1,256,16]{1,2,0:T(8,128)S(1)}, f32[1,256,16]{1,2,0:T(8,128)}, u32[]{:S(2)}) copy-start(f32[1,256,16]{1,2,0:T(8,128)} %param.17) | copy-start | bytes 49156
  14.1 16.3 %copy-start.16 = (bf16[1,256,256]{2,1,0:T(8,128)(2,1)S(1)}, bf16[1,256,256]{2,1,0:T(8,128)(2,1)}, u32[]{:S(2)}) copy-start(bf16[1,256,256]{2,1,0:T(8,128)(2,1)} %param.15) | copy-start | bytes 393220
  15.0 17.4 %copy-start.17 = (bf16[1,256,256]{2,1,0:T(8,128)(2,1)S(1)}, bf16[1,256,256]{2,1,0:T(8,128)(2,1)}, u32[]{:S(2)}) copy-start(bf16[1,256,256]{2,1,0:T(8,128)(2,1)} %param.16) | copy-start | bytes 393220
  15.0 28.3 %all-to-all-start.1 = ((bf16[2,2,65536]{2,1,0:T(2,128)(2,1)}), bf16[2,2,65536]{2,1,0:T(2,128)(2,1)S(1)}, u32[]{:S(2)}, u32[]{:S(2)}) async-start(bf16[2,2,65536]{2,1,0:T(2,128)(2,1)} %reshape.420), calls=%async_computation.1 | async-start | bytes 1048576 | tf_op jit(solution)/shard_map/all_to_all | solution.py:119
  25.6 31.9 %copy-start.25 = (f32[8]{0:T(128)}, f32[8]{0:T(128)S(1)}, u32[]{:S(2)}) copy-start(f32[8]{0:T(128)S(1)} %dynamic_slice.111) | copy-start | bytes 100
  25.6 31.8 %copy-start.27 = (f32[8]{0:T(128)}, f32[8]{0:T(128)S(1)}, u32[]{:S(2)}) copy-start(f32[8]{0:T(128)S(1)} %fusion.50) | copy-start | bytes 100
  43.3 7.0 all-to-all-start.2
  50.4 7.1 all-to-all-start
  53.6 797.8 %reduce-scatter.3.cloned.1.call-start = ((), (), s32[]{:S(2)}) async-start(), calls=%async_computation.7 | async-start | bytes 786432 | tf_op jit(solution)/shard_map/reduce_scatter | solution.py:156
  82.4 9.5 %copy-start.7 = (f32[256]{0:T(256)}, f32[256]{0:T(256)S(1)}, u32[]{:S(2)}) copy-start(f32[256]{0:T(256)S(1)} %get-tuple-element.923) | copy-start | bytes 3076 | tf_op jit(solution)/shard_map/transpose(jvp())/while
  83.5 8.5 copy-start.11
  99.4 5.3 copy-start.19
  99.4 5.3 copy-start.35
  113.2 9.5 %copy-start.7 = (f32[256]{0:T(256)}, f32[256]{0:T(256)S(1)}, u32[]{:S(2)}) copy-start(f32[256]{0:T(256)S(1)} %get-tuple-element.923) | copy-start | bytes 3076 | tf_op jit(solution)/shard_map/transpose(jvp())/while
  114.3 8.4 copy-start.11
  130.1 5.3 copy-start.19
  135.6 7.2 copy-start.4
  135.6 717.4 %reduce-scatter.5.cloned.1.call-start = ((), (), s32[]{:S(2)}) async-start(), calls=%async_computation.8 | async-start | bytes 786432 | tf_op jit(solution)/shard_map/reduce_scatter | solution.py:157
  139.2 9.7 %all-to-all-start.4 = ((f32[2,1,2048]{2,1,0:T(1,128)}), f32[2,1,2048]{2,1,0:T(1,128)S(1)}, u32[]{:S(2)}, u32[]{:S(2)}) async-start(f32[2,1,2048]{2,1,0:T(1,128)} %reshape.426), calls=%async_computation.6 | async-start | bytes 32768 | tf_op jit(solution)/shard_map/all_to_all | solution.py:154
  148.9 5.4 all-to-all-start.3
  (37 other events, 73.1 us)
Sparse Core Ops, SparseCore 0:
  135.7 16.2 reduce-scatter.2
  155.0 17.3 reduce-scatter.4
